TPU v7x, 32 devices: a whole 2x2x4 slice. The times are simulated.
32 devices in a mesh: row: 4 (over x, core), col: 8 (over z, y).
Axes of the slice: x: 2, y: 2, z: 4, core: 2. Of those that a mesh axis runs over, the one named last changes fastest.
Arguments:
- points: bfloat16 [65536, 256], P(('row', 'col')), may hold values from -6 to 6
- rotated_slot: int32 [65536], P(('row', 'col')), may hold values from 0 to 65535, as said below
- fine_attend_in: bfloat16 [2, 256, 768], replicated, may hold values from -8 to 8
- fine_attend_out: bfloat16 [2, 256, 256], replicated, may hold values from -0.375 to 0.375
- fine_gate_up: bfloat16 [2, 256, 2048], replicated, may hold values from -0.375 to 0.375
- fine_down: bfloat16 [2, 1024, 256], replicated, may hold values from -0.1875 to 0.1875
- pool_weight: bfloat16 [2048, 512], replicated, may hold values from -0.125 to 0.125
- coarse_attend_in: bfloat16 [512, 1536], replicated, may hold values from -8 to 8
- coarse_attend_out: bfloat16 [512, 512], replicated, may hold values from -0.25 to 0.25
- coarse_gate_up: bfloat16 [512, 4096], replicated, may hold values from -0.25 to 0.25
- coarse_down: bfloat16 [2048, 512], replicated, may hold values from -0.125 to 0.125
- unpool_weight: bfloat16 [512, 2048], replicated, may hold values from -0.25 to 0.25
Outputs:
- refined: bfloat16 [65536, 256], P(('row', 'col'))
Inputs may be any that keep to these rules, and one draw needn't show every extreme that they name: rotated_slot is a permutation of all points; each point's rotated position lies on a device with the same col index; of the points of one device at most 1280 have rotated positions on any one device, and in every col group some device sends exactly 1280 to one device.
All inputs are finite; a program needn't handle non-finite values.
Results may differ from a plain program's by a relative error of at most 0.017.
Values may be sent and summed in bfloat16 or wider, within the bound.
A program may use at most 128 MiB of HBM per device.

v0:
```python
import functools
import math

import jax
import jax.numpy as jnp
from jax import lax
from jax.experimental import pallas as pl
from jax.experimental.pallas import tpu as pltpu
from jax.sharding import PartitionSpec as P

HEADS = 8
CHEADS = 8
BALL = 256
GROUP = 8
FAN = 8
LANES = 128
EPS = 1e-06
F32 = jnp.float32
BF16 = jnp.bfloat16
LOG2E = 1.4426950408889634


def dot(a, b):
    return jnp.dot(a, b, preferred_element_type=F32)


def dot_t(a, b):
    return lax.dot_general(a, b, (((1,), (1,)), ((), ())), preferred_element_type=F32)


def normed(x):
    wide = x.astype(F32)
    return (wide * lax.rsqrt(jnp.mean(wide * wide, axis=-1, keepdims=True) + EPS)).astype(BF16)


def ff_sum(x, gate_up, down):
    both = dot(normed(x), gate_up)
    half = both.shape[1] // 2
    g = both[:, :half]
    hidden = ((0.5 * g) * (1.0 + jnp.tanh(0.5 * g)) * both[:, half:]).astype(BF16)
    return x.astype(F32) + dot(hidden, down)


def fine_attention(u, w_in, w_out):
    rows, width = u.shape
    packed = dot(normed(u), w_in).astype(BF16)
    q, k, v = packed[:, :width], packed[:, width:2 * width], packed[:, 2 * width:]
    size = width // HEADS
    factor = size ** -0.5 * LOG2E
    head_of = lax.broadcasted_iota(jnp.int32, (rows, width), 1) // size
    zero = jnp.zeros((), BF16)
    weights, values = [], []
    for h in range(HEADS):
        mine = head_of == h
        s = dot_t(jnp.where(mine, q, zero), k)
        m = jnp.max(s, axis=-1, keepdims=True)
        weights.append(jnp.exp2((s - m) * factor).astype(BF16))
        values.append(
            jnp.concatenate(
                (jnp.where(mine, v, zero), jnp.where(mine, jnp.ones((), BF16), zero)), axis=1
            )
        )
    both = dot(jnp.concatenate(weights, axis=1), jnp.concatenate(values, axis=0))
    mixture = (both[:, :width] / both[:, width:]).astype(BF16)
    return dot(mixture, w_out)


def row_peers():
    me = lax.axis_index("row")
    near = me + 1 - 2 * (me % 2)
    far = me + 2 - 4 * ((me // 2) % 2)
    return me, near, far


def greet(peers, axis):
    barrier = pltpu.get_barrier_semaphore()
    for peer in peers:
        pl.semaphore_signal(
            barrier, inc=1, device_id={axis: peer}, device_id_type=pl.DeviceIdType.MESH
        )
    pl.semaphore_wait(barrier, len(peers))


class RowGather:
    def __init__(self, out, chunk, send, recv):
        self.out, self.chunk, self.send, self.recv = out, chunk, send, recv
        self.me, self.near, self.far = row_peers()

    def copy(self, kind, c, block, peer):
        spot = self.out.at[block, pl.ds(c * self.chunk, self.chunk)]
        return pltpu.make_async_remote_copy(
            src_ref=spot,
            dst_ref=spot,
            send_sem=self.send.at[kind, c],
            recv_sem=self.recv.at[kind, c],
            device_id={"row": peer},
            device_id_type=pl.DeviceIdType.MESH,
        )

    def own(self, c):
        self.copy(0, c, self.me, self.far).start()
        self.copy(1, c, self.me, self.near).start()

    def relay(self, c):
        self.copy(0, c, self.far, self.far).wait_recv()
        self.copy(2, c, self.far, self.near).start()

    def finish(self, c):
        self.copy(0, c, self.me, self.far).wait_send()
        self.copy(1, c, self.me, self.near).wait_send()
        self.copy(2, c, self.far, self.near).wait_send()
        self.copy(1, c, self.near, self.near).wait_recv()
        self.copy(2, c, self.far + self.near - self.me, self.near).wait_recv()


LAG = 2


def layer_one_kernel(
    col_size, points, slots, w_in, w_out, gate_up, down, out, inverse, slot_all, send, recv,
    s_send, s_recv,
):
    rows = points.shape[0]
    count = rows // BALL
    me, near, far = row_peers()
    other = far + near - me
    greet((near, far, other), "row")
    slot_all[me] = slots[...]

    def slot_copy(kind, block, peer):
        return pltpu.make_async_remote_copy(
            src_ref=slots,
            dst_ref=slot_all.at[block],
            send_sem=s_send.at[kind],
            recv_sem=s_recv.at[kind],
            device_id={"row": peer},
            device_id_type=pl.DeviceIdType.MESH,
        )

    for kind, peer in enumerate((near, far, other)):
        slot_copy(kind, me, peer).start()
    gather = RowGather(out, BALL, send, recv)

    def step(b, carry):
        u = points[pl.ds(b * BALL, BALL), :]
        mixed = (u.astype(F32) + fine_attention(u, w_in[...], w_out[...])).astype(BF16)
        out[me, pl.ds(b * BALL, BALL), :] = ff_sum(mixed, gate_up[...], down[...]).astype(BF16)
        gather.own(b)

        @pl.when(b >= LAG)
        def _():
            gather.relay(b - LAG)

        return carry

    lax.fori_loop(0, count, step, 0)
    for kind, peer in enumerate((near, far, other)):
        slot_copy(kind, peer, peer).wait()
    lines, lanes = slots.shape
    row_id = lax.broadcasted_iota(jnp.int32, (lines, lanes), 0)
    lane_id = lax.broadcasted_iota(jnp.int32, (lines, lanes), 1).astype(F32)
    sub_id = lax.broadcasted_iota(jnp.int32, (lanes, lanes), 0)
    left, right = [], []
    for r in range(slot_all.shape[0]):
        for c in range(lines):
            line = slot_all[r, c:c + 1, :]
            line = jnp.where(line // (rows * col_size) == me, line % rows, rows)
            hit = row_id == line // lanes
            left.append(
                jnp.concatenate(
                    (jnp.where(hit, float(r * lines + c), 0.0), jnp.where(hit, lane_id, 0.0)),
                    axis=0,
                ).astype(BF16)
            )
            right.append(jnp.where(sub_id == line % lanes, 1.0, 0.0).astype(BF16))
    found = dot_t(jnp.concatenate(left, axis=1), jnp.concatenate(right, axis=1))
    inverse[...] = (found[:lines] * lanes + found[lines:]).astype(jnp.int32)

    def tail(c, carry):
        gather.relay(c)
        return carry

    lax.fori_loop(max(count - LAG, 0), count, tail, 0)

    def end(c, carry):
        gather.finish(c)
        return carry

    lax.fori_loop(0, count, end, 0)


def widen(source, wide):
    rows = source.shape[1]
    for block in range(source.shape[0]):

        def step(i, carry):
            at = pl.multiple_of(i * BALL, BALL)
            wide[pl.ds(block * rows + at, BALL), :] = source[
                block, pl.ds(at, BALL), :
            ].astype(F32)
            return carry

        lax.fori_loop(0, rows // BALL, step, 0)


def take_rows(wide, index, base, taken):
    unit = 32

    def step(i, carry):
        for j in range(unit):
            at = i * unit + j
            taken[pl.ds(at, 1), :] = wide[pl.ds(index[base + at], 1), :]
        return carry

    lax.fori_loop(0, taken.shape[0] // unit, step, 0)


def turn_kernel(first, index, w_in, w_out, out, wide, taken, send, recv):
    rows = first.shape[1]
    count = rows // BALL
    me, near, far = row_peers()
    greet((near, far), "row")
    gather = RowGather(out, BALL, send, recv)
    widen(first, wide)

    def step(b, carry):
        take_rows(wide, index, b * BALL, taken)
        u = taken[...].astype(BF16)
        out[me, pl.ds(b * BALL, BALL), :] = fine_attention(u, w_in[...], w_out[...]).astype(BF16)
        gather.own(b)

        @pl.when(b >= LAG)
        def _():
            gather.relay(b - LAG)

        return carry

    lax.fori_loop(0, count, step, 0)

    def tail(c, carry):
        gather.relay(c)
        return carry

    lax.fori_loop(max(count - LAG, 0), count, tail, 0)

    def end(c, carry):
        gather.finish(c)
        return carry

    lax.fori_loop(0, count, end, 0)


def layer_two_kernel(
    first, turned, index, gate_up, down, pool, second, pooled, wide, taken, tall, send, recv
):
    rows = second.shape[0]
    count = rows // BALL
    small = BALL // FAN
    col = lax.axis_index("col")
    me = col % GROUP
    base = col - me
    me_row = lax.axis_index("row")
    flip = me + 1 - 2 * (me % 2)
    peers = [(me + 2 * step) % GROUP for step in range(1, GROUP // 2)]
    greet([base + p for p in [flip] + peers], "col")
    widen(turned, wide)
    pieces = recv.shape[1]
    piece = pooled.shape[1] // pieces
    per = count // pieces

    def copy(kind, c, block, peer):
        spot = pooled.at[block, pl.ds(c * piece, piece)]
        return pltpu.make_async_remote_copy(
            src_ref=spot,
            dst_ref=spot,
            send_sem=send.at[kind, c],
            recv_sem=recv.at[kind, c],
            device_id={"col": base + peer},
            device_id_type=pl.DeviceIdType.MESH,
        )

    lead = GROUP // 2

    def source_of(kind):
        return (me + GROUP - 2 * kind) % GROUP

    def step(c, carry):
        def ball(i, carry):
            b = c * per + i
            at = pl.multiple_of(b * BALL, BALL)
            take_rows(wide, index, b * BALL, taken)
            mixed = (
                first[me_row, pl.ds(at, BALL), :].astype(F32) + taken[...]
            ).astype(BF16)
            result = ff_sum(mixed, gate_up[...], down[...]).astype(BF16)
            second[pl.ds(at, BALL), :] = result
            for t in range(tall.shape[0]):
                tall[t, pl.ds(pl.multiple_of(i * BALL, BALL), BALL), :] = result[
                    :, t * LANES:(t + 1) * LANES
                ].astype(F32)
            return carry

        lax.fori_loop(0, per, ball, 0)
        side = [
            tall[t, pl.ds(j, piece, stride=FAN), :].astype(BF16)
            for j in range(FAN)
            for t in range(tall.shape[0])
        ]
        total = dot(jnp.concatenate(side, axis=1), pool[...])
        pooled[me, pl.ds(pl.multiple_of(c * piece, piece), piece), :] = total.astype(BF16)
        copy(0, c, me, flip).start()
        for kind in range(1, lead):
            copy(kind, c, me, peers[kind - 1]).start()
        return carry

    lax.fori_loop(0, pieces, step, 0)

    def relay(c, carry):
        for kind in range(1, lead):
            copy(kind, c, source_of(kind), peers[0]).wait_recv()
            copy(lead - 1 + kind, c, source_of(kind), flip).start()
        return carry

    lax.fori_loop(0, pieces, relay, 0)

    def end(c, carry):
        copy(0, c, me, flip).wait_send()
        copy(0, c, flip, flip).wait_recv()
        for kind in range(1, lead):
            copy(kind, c, me, peers[kind - 1]).wait_send()
            copy(lead - 1 + kind, c, source_of(kind), flip).wait_send()
            origin = source_of(kind)
            copy(lead - 1 + kind, c, origin + 1 - 2 * (origin % 2), flip).wait_recv()
        return carry

    lax.fori_loop(0, pieces, end, 0)


def coarse_kernel(
    pooled, second, w_in, w_out, gate_up, down, unpool, out, keys, values, lifted
):
    me = lax.axis_index("col") % GROUP
    own = pooled[me]
    rows, width = own.shape
    size = width // CHEADS
    factor = size ** -0.5 * LOG2E
    for block in range(GROUP):
        packed = dot(normed(pooled[block]), w_in[:, width:]).astype(BF16)
        keys[pl.ds(block * rows, rows), :] = packed[:, :width]
        values[pl.ds(block * rows, rows), :] = packed[:, width:]
    q = dot(normed(own), w_in[:, :width]).astype(BF16)
    part = 256
    head_of = lax.broadcasted_iota(jnp.int32, (rows, part), 1) // size
    zero = jnp.zeros((), BF16)
    mixture = []
    for g in range(width // part):
        at = g * part
        acc = jnp.zeros((rows, part), F32)
        for h in range(part // size):
            mine = head_of == h
            s = dot_t(jnp.where(mine, q[:, at:at + part], zero), keys[:, at:at + part])
            m = jnp.max(s, axis=-1, keepdims=True)
            e = jnp.exp2((s - m) * factor)
            r = dot(e.astype(BF16), values[:, at:at + part])
            acc = jnp.where(mine, r / jnp.sum(e, axis=-1, keepdims=True), acc)
        mixture.append(acc.astype(BF16))
    mixed = (own.astype(F32) + dot(jnp.concatenate(mixture, axis=1), w_out[...])).astype(BF16)
    coarse = ff_sum(mixed, gate_up[...], down[...]).astype(BF16)
    up = normed(coarse)
    fine = out.shape[1]
    for j in range(FAN):
        part_up = dot(up, unpool[:, j * fine:(j + 1) * fine])
        for t in range(lifted.shape[0]):
            lifted[t, pl.ds(j, rows, stride=FAN), :] = part_up[:, t * LANES:(t + 1) * LANES]
    for c in range(out.shape[0] // BALL):
        at = c * BALL
        for t in range(lifted.shape[0]):
            lane = slice(t * LANES, (t + 1) * LANES)
            out[at:at + BALL, lane] = (
                second[at:at + BALL, lane].astype(F32) + lifted[t, at:at + BALL, :]
            ).astype(BF16)


VMEM = pl.BlockSpec(memory_space=pltpu.VMEM)
SMEM = pl.BlockSpec(memory_space=pltpu.SMEM)
DMA = pltpu.SemaphoreType.DMA


def local(
    points,
    rotated_slot,
    fine_attend_in,
    fine_attend_out,
    fine_gate_up,
    fine_down,
    pool_weight,
    coarse_attend_in,
    coarse_attend_out,
    coarse_gate_up,
    coarse_down,
    unpool_weight,
):
    rows, width = points.shape
    row_size = lax.axis_size("row")
    col_size = lax.axis_size("col")
    count = rows // BALL
    small = rows // FAN
    coarse_width = pool_weight.shape[1]
    lanes = LANES
    lines = rows // lanes
    grant = 48 * 1024 * 1024
    everyone = jax.ShapeDtypeStruct((row_size, rows, width), BF16)

    first, inverse = pl.pallas_call(
        functools.partial(layer_one_kernel, col_size),
        out_shape=(everyone, jax.ShapeDtypeStruct((lines, lanes), jnp.int32)),
        in_specs=[VMEM] * 6,
        out_specs=(VMEM, VMEM),
        scratch_shapes=[
            pltpu.VMEM((row_size, lines, lanes), jnp.int32),
            DMA((3, count)),
            DMA((3, count)),
            DMA((3,)),
            DMA((3,)),
        ],
        compiler_params=pltpu.CompilerParams(
            collective_id=0, has_side_effects=True, vmem_limit_bytes=grant
        ),
        name="layer_one",
    )(
        points,
        rotated_slot.reshape(lines, lanes),
        fine_attend_in[0],
        fine_attend_out[0],
        fine_gate_up[0],
        fine_down[0],
    )

    turned = pl.pallas_call(
        turn_kernel,
        out_shape=everyone,
        in_specs=[VMEM, SMEM, VMEM, VMEM],
        out_specs=VMEM,
        scratch_shapes=[
            pltpu.VMEM((row_size * rows, width), F32),
            pltpu.VMEM((BALL, width), F32),
            DMA((3, count)),
            DMA((3, count)),
        ],
        compiler_params=pltpu.CompilerParams(
            collective_id=1, has_side_effects=True, vmem_limit_bytes=grant
        ),
        name="turn",
    )(first, inverse.reshape(-1), fine_attend_in[1], fine_attend_out[1])

    target = rotated_slot // (rows * col_size)
    index = target * rows + rotated_slot % rows
    pieces = 2
    kinds = GROUP - 1
    second, pooled = pl.pallas_call(
        layer_two_kernel,
        out_shape=(
            jax.ShapeDtypeStruct((rows, width), BF16),
            jax.ShapeDtypeStruct((GROUP, small, coarse_width), BF16),
        ),
        in_specs=[VMEM, VMEM, SMEM, VMEM, VMEM, VMEM],
        out_specs=(VMEM, VMEM),
        scratch_shapes=[
            pltpu.VMEM((row_size * rows, width), F32),
            pltpu.VMEM((BALL, width), F32),
            pltpu.VMEM((width // LANES, rows // pieces, LANES), F32),
            DMA((kinds, pieces)),
            DMA((kinds, pieces)),
        ],
        compiler_params=pltpu.CompilerParams(
            collective_id=2, has_side_effects=True, vmem_limit_bytes=grant
        ),
        name="layer_two",
    )(first, turned, index, fine_gate_up[1], fine_down[1], pool_weight)

    return pl.pallas_call(
        coarse_kernel,
        out_shape=jax.ShapeDtypeStruct((rows, width), BF16),
        in_specs=[VMEM] * 7,
        out_specs=VMEM,
        scratch_shapes=[
            pltpu.VMEM((GROUP * small, coarse_width), BF16),
            pltpu.VMEM((GROUP * small, coarse_width), BF16),
            pltpu.VMEM((width // LANES, rows, LANES), F32),
        ],
        compiler_params=pltpu.CompilerParams(vmem_limit_bytes=grant),
        name="coarse",
    )(
        pooled,
        second,
        coarse_attend_in,
        coarse_attend_out,
        coarse_gate_up,
        coarse_down,
        unpool_weight,
    )


def solution(mesh):
    split = P(("row", "col"), None)
    placed = (split, P(("row", "col"))) + (P(),) * 10
    return jax.shard_map(local, mesh=mesh, in_specs=placed, out_specs=split, check_vma=False)
```

profile of v0, /device:TPU:0, one launch (start us, length us, event | category | flops | bytes accessed | tf_op | source)
XLA Modules:
  0.0 132.3 jit_solution(2743669881468357853)
XLA Ops:
  0.0 0.0 copy-start.6
  0.0 0.8 fusion.2.index
  0.8 0.0 copy-start.5
  0.8 1.1 slice_bitcast_fusion.6
  2.0 1.2 slice_bitcast_fusion.4
  3.1 0.0 copy-done.6
  3.1 0.1 slice_bitcast_fusion.2
  3.2 0.0 copy-done.5
  3.2 0.0 copy-start.2
  3.2 0.0 copy-start.4
  3.2 0.1 slice_bitcast_fusion
  3.4 1.1 copy-done.2
  4.5 0.0 copy-done.4
  4.5 32.6 %layer_one.1 = (bf16[4,2048,256]{2,1,0:T(8,128)(2,1)}, s32[16,128]{1,0:T(8,128)S(1)}) custom-call(bf16[2048,256]{1,0:T(8,128)(2,1)S(1)} %copy-done.2, s32[16,128]{1,0:T(8,128)S(1)} %bitcast.18, bf16[256,768]{1,0:T(8,128)(2,1)S(1)} %get-tuple-element.18.w_in, bf16[256,256]{1,0:T(8,128)(2,1)S(1)} %get-tuple-element.20.w_out, ...), custom_call_target="tpu_custom_call" | custom-call | tf_op jit(solution)/shard_map/layer_one/pallas_call | solution.py:414
  37.0 32.1 %turn.1.turned = bf16[4,2048,256]{2,1,0:T(8,128)(2,1)S(1)} custom-call(bf16[4,2048,256]{2,1,0:T(8,128)(2,1)} %get-tuple-element.9.first, s32[2048]{0:T(1024)S(1)} %bitcast.19, bf16[256,768]{1,0:T(8,128)(2,1)S(1)} %get-tuple-element.17.w_in, bf16[256,256]{1,0:T(8,128)(2,1)S(1)} %get-tuple-element.19.w_out), custom_call_target="tpu_custom_call" | custom-call | tf_op jit(solution)/shard_map/turn/pallas_call | solution.py:439
  69.1 0.0 copy-start
  69.1 2.0 %copy-done = bf16[4,2048,256]{2,1,0:T(8,128)(2,1)} copy-done((bf16[4,2048,256]{2,1,0:T(8,128)(2,1)}, bf16[4,2048,256]{2,1,0:T(8,128)(2,1)S(1)}, u32[]{:S(2)}) %copy-start) | copy-done | bytes 4194328
  71.1 0.0 copy-start.1
  71.1 0.0 copy-start.3
  71.1 45.6 %layer_two.1 = (bf16[2048,256]{1,0:T(8,128)(2,1)S(1)}, bf16[8,256,512]{2,1,0:T(8,128)(2,1)S(1)}) custom-call(bf16[4,2048,256]{2,1,0:T(8,128)(2,1)} %get-tuple-element.9.first, bf16[4,2048,256]{2,1,0:T(8,128)(2,1)} %copy-done, s32[2048]{0:T(1024)S(1)} %fusion.2.index, bf16[256,2048]{1,0:T(8,128)(2,1)S(1)} %get-tuple-element.13.gate_up, ...), custom_call_target="tpu_custom_call" | custom-call | tf_op jit(solution)/shard_map/layer_two/pallas_call | solution.py:460
  116.7 0.0 copy-done.1
  116.7 0.0 copy-done.3
  116.7 15.6 %coarse.1 = bf16[2048,256]{1,0:T(8,128)(2,1)} custom-call(bf16[8,256,512]{2,1,0:T(8,128)(2,1)S(1)} %get-tuple-element.11.pooled, bf16[2048,256]{1,0:T(8,128)(2,1)S(1)} %get-tuple-element.12.second, bf16[512,1536]{1,0:T(8,128)(2,1)S(1)} %copy-done.1, bf16[512,512]{1,0:T(8,128)(2,1)S(1)} %copy-done.3, bf16[512,4096]{1,0:T(8,128)(2,1)} %gate_up.1, ...), custom_call_target="tpu_custom_call" | custom-call | tf_op jit(solution)/shard_map/coarse/pallas_call | solution.py:481
Async XLA Ops:
  0.0 3.1 %copy-start.6 = (bf16[2,1024,256]{2,1,0:T(8,128)(2,1)S(1)}, bf16[2,1024,256]{2,1,0:T(8,128)(2,1)}, u32[]{:S(2)}) copy-start(bf16[2,1024,256]{2,1,0:T(8,128)(2,1)} %param.17) | copy-start | bytes 3145732
  0.8 2.4 %copy-start.5 = (bf16[2,256,2048]{2,1,0:T(8,128)(2,1)S(1)}, bf16[2,256,2048]{2,1,0:T(8,128)(2,1)}, u32[]{:S(2)}) copy-start(bf16[2,256,2048]{2,1,0:T(8,128)(2,1)} %param.16) | copy-start | bytes 6291460
  3.2 1.2 copy-start.2
  3.2 1.2 copy-start.4
  69.1 2.0 %copy-start = (bf16[4,2048,256]{2,1,0:T(8,128)(2,1)}, bf16[4,2048,256]{2,1,0:T(8,128)(2,1)S(1)}, u32[]{:S(2)}) copy-start(bf16[4,2048,256]{2,1,0:T(8,128)(2,1)S(1)} %turn.1.turned) | copy-start | bytes 12582916
  71.1 45.6 %copy-start.1 = (bf16[512,1536]{1,0:T(8,128)(2,1)S(1)}, bf16[512,1536]{1,0:T(8,128)(2,1)}, u32[]{:S(2)}) copy-start(bf16[512,1536]{1,0:T(8,128)(2,1)} %w_in.1) | copy-start | bytes 4718596
  71.1 45.7 %copy-start.3 = (bf16[512,512]{1,0:T(8,128)(2,1)S(1)}, bf16[512,512]{1,0:T(8,128)(2,1)}, u32[]{:S(2)}) copy-start(bf16[512,512]{1,0:T(8,128)(2,1)} %w_out.1) | copy-start | bytes 1572868
where the time goes:
time: 133 us; the launch traced here: 132 us
  Pallas kernels  126 us (95%)
  local copies, waits for them, and re-layouts  5.55 us (4%)
    pallas_call x1, Pallas kernels, local(): pl.pallas_call(layer_two_kernel, out_shape=(jax.ShapeDtypeStruct((rows, w...  45.6 us
    pallas_call x1, Pallas kernels, local(): pl.pallas_call(functools.partial(layer_one_kernel, col_size), out_shape=(...  32.6 us
    pallas_call x1, Pallas kernels, local(): pl.pallas_call(turn_kernel, out_shape=everyone, in_specs=[VMEM, SMEM, VME...  32.1 us
    pallas_call x1, Pallas kernels, local(): pl.pallas_call(coarse_kernel, out_shape=jax.ShapeDtypeStruct((rows, width...  15.6 us
    unnamed x14, local copies, waits for them, and re-layouts  3.04 us

commit v1 on v0

--- a/solution.py
+++ b/solution.py
@@ -82,12 +82,14 @@
 
 
 class RowGather:
-    def __init__(self, out, chunk, send, recv):
-        self.out, self.chunk, self.send, self.recv = out, chunk, send, recv
+    def __init__(self, held, wide, chunk, send, recv):
+        self.held, self.wide, self.chunk = held, wide, chunk
+        self.send, self.recv = send, recv
         self.me, self.near, self.far = row_peers()
+        self.last = self.far + self.near - self.me
 
     def copy(self, kind, c, block, peer):
-        spot = self.out.at[block, pl.ds(c * self.chunk, self.chunk)]
+        spot = self.held.at[block, pl.ds(c * self.chunk, self.chunk)]
         return pltpu.make_async_remote_copy(
             src_ref=spot,
             dst_ref=spot,
@@ -97,28 +99,69 @@
             device_id_type=pl.DeviceIdType.MESH,
         )
 
-    def own(self, c):
+    def widen(self, block, c):
+        rows = self.held.shape[1]
+        at = pl.multiple_of(block * rows + c * self.chunk, self.chunk)
+        self.wide[pl.ds(at, self.chunk), :] = self.held[
+            block, pl.ds(pl.multiple_of(c * self.chunk, self.chunk), self.chunk), :
+        ].astype(F32)
+
+    def own(self, c, value):
+        at = pl.multiple_of(c * self.chunk, self.chunk)
+        self.held[self.me, pl.ds(at, self.chunk), :] = value
         self.copy(0, c, self.me, self.far).start()
         self.copy(1, c, self.me, self.near).start()
+        self.widen(self.me, c)
 
     def relay(self, c):
         self.copy(0, c, self.far, self.far).wait_recv()
         self.copy(2, c, self.far, self.near).start()
-
-    def finish(self, c):
-        self.copy(0, c, self.me, self.far).wait_send()
-        self.copy(1, c, self.me, self.near).wait_send()
-        self.copy(2, c, self.far, self.near).wait_send()
+        self.widen(self.far, c)
         self.copy(1, c, self.near, self.near).wait_recv()
-        self.copy(2, c, self.far + self.near - self.me, self.near).wait_recv()
+        self.widen(self.near, c)
+
+    def arrive(self, c):
+        self.copy(2, c, self.last, self.near).wait_recv()
+        self.widen(self.last, c)
+
+    def inside(self, b):
+        @pl.when(b >= LAG)
+        def _():
+            self.relay(b - LAG)
+
+        @pl.when(b >= LAG + 1)
+        def _():
+            self.arrive(b - LAG - 1)
+
+    def finish(self, count):
+        def tail(c, carry):
+            self.relay(c)
+
+            @pl.when(c >= 1)
+            def _():
+                self.arrive(c - 1)
+
+            return carry
+
+        lax.fori_loop(max(count - LAG, 0), count, tail, 0)
+        self.arrive(count - 1)
+
+        def end(c, carry):
+            self.copy(0, c, self.me, self.far).wait_send()
+            self.copy(1, c, self.me, self.near).wait_send()
+            self.copy(2, c, self.far, self.near).wait_send()
+            return carry
+
+        lax.fori_loop(0, count, end, 0)
 
 
 LAG = 2
+COL_LAG = 3
 
 
 def layer_one_kernel(
-    col_size, points, slots, w_in, w_out, gate_up, down, out, inverse, slot_all, send, recv,
-    s_send, s_recv,
+    col_size, points, slots, w_in, w_out, gate_up, down, out, wide, inverse, route, held,
+    slot_all, send, recv, s_send, s_recv,
 ):
     rows = points.shape[0]
     count = rows // BALL
@@ -139,18 +182,16 @@
 
     for kind, peer in enumerate((near, far, other)):
         slot_copy(kind, me, peer).start()
-    gather = RowGather(out, BALL, send, recv)
+    route[...] = slots[...] // (rows * col_size) * rows + slots[...] % rows
+    gather = RowGather(held, wide, BALL, send, recv)
 
     def step(b, carry):
         u = points[pl.ds(b * BALL, BALL), :]
-        mixed = (u.astype(F32) + fine_attention(u, w_in[...], w_out[...])).astype(BF16)
-        out[me, pl.ds(b * BALL, BALL), :] = ff_sum(mixed, gate_up[...], down[...]).astype(BF16)
-        gather.own(b)
-
-        @pl.when(b >= LAG)
-        def _():
-            gather.relay(b - LAG)
-
+        mixed = (u.astype(F32) + fine_attention(u, w_in[0], w_out[0])).astype(BF16)
+        value = ff_sum(mixed, gate_up[0], down[0]).astype(BF16)
+        out[pl.ds(pl.multiple_of(b * BALL, BALL), BALL), :] = value
+        gather.own(b, value)
+        gather.inside(b)
         return carry
 
     lax.fori_loop(0, count, step, 0)
@@ -176,31 +217,7 @@
     found = dot_t(jnp.concatenate(left, axis=1), jnp.concatenate(right, axis=1))
     inverse[...] = (found[:lines] * lanes + found[lines:]).astype(jnp.int32)
 
-    def tail(c, carry):
-        gather.relay(c)
-        return carry
-
-    lax.fori_loop(max(count - LAG, 0), count, tail, 0)
-
-    def end(c, carry):
-        gather.finish(c)
-        return carry
-
-    lax.fori_loop(0, count, end, 0)
-
-
-def widen(source, wide):
-    rows = source.shape[1]
-    for block in range(source.shape[0]):
-
-        def step(i, carry):
-            at = pl.multiple_of(i * BALL, BALL)
-            wide[pl.ds(block * rows + at, BALL), :] = source[
-                block, pl.ds(at, BALL), :
-            ].astype(F32)
-            return carry
-
-        lax.fori_loop(0, rows // BALL, step, 0)
+    gather.finish(count)
 
 
 def take_rows(wide, index, base, taken):
@@ -215,43 +232,27 @@
     lax.fori_loop(0, taken.shape[0] // unit, step, 0)
 
 
-def turn_kernel(first, index, w_in, w_out, out, wide, taken, send, recv):
-    rows = first.shape[1]
+def turn_kernel(source, index, w_in, w_out, wide, held, taken, send, recv):
+    rows = held.shape[1]
     count = rows // BALL
     me, near, far = row_peers()
     greet((near, far), "row")
-    gather = RowGather(out, BALL, send, recv)
-    widen(first, wide)
+    gather = RowGather(held, wide, BALL, send, recv)
 
     def step(b, carry):
-        take_rows(wide, index, b * BALL, taken)
+        take_rows(source, index, b * BALL, taken)
         u = taken[...].astype(BF16)
-        out[me, pl.ds(b * BALL, BALL), :] = fine_attention(u, w_in[...], w_out[...]).astype(BF16)
-        gather.own(b)
-
-        @pl.when(b >= LAG)
-        def _():
-            gather.relay(b - LAG)
-
+        gather.own(b, fine_attention(u, w_in[1], w_out[1]).astype(BF16))
+        gather.inside(b)
         return carry
 
     lax.fori_loop(0, count, step, 0)
 
-    def tail(c, carry):
-        gather.relay(c)
-        return carry
-
-    lax.fori_loop(max(count - LAG, 0), count, tail, 0)
-
-    def end(c, carry):
-        gather.finish(c)
-        return carry
-
-    lax.fori_loop(0, count, end, 0)
+    gather.finish(count)
 
 
 def layer_two_kernel(
-    first, turned, index, gate_up, down, pool, second, pooled, wide, taken, tall, send, recv
+    first, wide, index, gate_up, down, pool, second, pooled, taken, tall, send, recv
 ):
     rows = second.shape[0]
     count = rows // BALL
@@ -259,11 +260,9 @@
     col = lax.axis_index("col")
     me = col % GROUP
     base = col - me
-    me_row = lax.axis_index("row")
     flip = me + 1 - 2 * (me % 2)
     peers = [(me + 2 * step) % GROUP for step in range(1, GROUP // 2)]
     greet([base + p for p in [flip] + peers], "col")
-    widen(turned, wide)
     pieces = recv.shape[1]
     piece = pooled.shape[1] // pieces
     per = count // pieces
@@ -290,9 +289,9 @@
             at = pl.multiple_of(b * BALL, BALL)
             take_rows(wide, index, b * BALL, taken)
             mixed = (
-                first[me_row, pl.ds(at, BALL), :].astype(F32) + taken[...]
+                first[pl.ds(at, BALL), :].astype(F32) + taken[...]
             ).astype(BF16)
-            result = ff_sum(mixed, gate_up[...], down[...]).astype(BF16)
+            result = ff_sum(mixed, gate_up[1], down[1]).astype(BF16)
             second[pl.ds(at, BALL), :] = result
             for t in range(tall.shape[0]):
                 tall[t, pl.ds(pl.multiple_of(i * BALL, BALL), BALL), :] = result[
@@ -311,9 +310,12 @@
         copy(0, c, me, flip).start()
         for kind in range(1, lead):
             copy(kind, c, me, peers[kind - 1]).start()
+
+        @pl.when(c >= COL_LAG)
+        def _():
+            relay(c - COL_LAG, 0)
+
         return carry
-
-    lax.fori_loop(0, pieces, step, 0)
 
     def relay(c, carry):
         for kind in range(1, lead):
@@ -321,7 +323,8 @@
             copy(lead - 1 + kind, c, source_of(kind), flip).start()
         return carry
 
-    lax.fori_loop(0, pieces, relay, 0)
+    lax.fori_loop(0, pieces, step, 0)
+    lax.fori_loop(max(pieces - COL_LAG, 0), pieces, relay, 0)
 
     def end(c, carry):
         copy(0, c, me, flip).wait_send()
@@ -408,15 +411,25 @@
     coarse_width = pool_weight.shape[1]
     lanes = LANES
     lines = rows // lanes
-    grant = 48 * 1024 * 1024
-    everyone = jax.ShapeDtypeStruct((row_size, rows, width), BF16)
-
-    first, inverse = pl.pallas_call(
+    mib = 1024 * 1024
+    everyone = jax.ShapeDtypeStruct((row_size * rows, width), F32)
+    held = pltpu.VMEM((row_size, rows, width), BF16)
+    scalars = jax.ShapeDtypeStruct((lines, lanes), jnp.int32)
+
+    first, wide, inverse, route = pl.pallas_call(
         functools.partial(layer_one_kernel, col_size),
-        out_shape=(everyone, jax.ShapeDtypeStruct((lines, lanes), jnp.int32)),
-        in_specs=[VMEM] * 6,
-        out_specs=(VMEM, VMEM),
+        out_shape=(jax.ShapeDtypeStruct((rows, width), BF16), everyone, scalars, scalars),
+        in_specs=[
+            VMEM,
+            VMEM,
+            VMEM,
+            VMEM,
+            VMEM,
+            VMEM,
+        ],
+        out_specs=(VMEM,) * 4,
         scratch_shapes=[
+            held,
             pltpu.VMEM((row_size, lines, lanes), jnp.int32),
             DMA((3, count)),
             DMA((3, count)),
@@ -424,16 +437,16 @@
             DMA((3,)),
         ],
         compiler_params=pltpu.CompilerParams(
-            collective_id=0, has_side_effects=True, vmem_limit_bytes=grant
+            collective_id=0, has_side_effects=True, vmem_limit_bytes=36 * mib
         ),
         name="layer_one",
     )(
         points,
         rotated_slot.reshape(lines, lanes),
-        fine_attend_in[0],
-        fine_attend_out[0],
-        fine_gate_up[0],
-        fine_down[0],
+        fine_attend_in,
+        fine_attend_out,
+        fine_gate_up,
+        fine_down,
     )
 
     turned = pl.pallas_call(
@@ -442,20 +455,18 @@
         in_specs=[VMEM, SMEM, VMEM, VMEM],
         out_specs=VMEM,
         scratch_shapes=[
-            pltpu.VMEM((row_size * rows, width), F32),
+            held,
             pltpu.VMEM((BALL, width), F32),
             DMA((3, count)),
             DMA((3, count)),
         ],
         compiler_params=pltpu.CompilerParams(
-            collective_id=1, has_side_effects=True, vmem_limit_bytes=grant
+            collective_id=1, has_side_effects=True, vmem_limit_bytes=32 * mib
         ),
         name="turn",
-    )(first, inverse.reshape(-1), fine_attend_in[1], fine_attend_out[1])
-
-    target = rotated_slot // (rows * col_size)
-    index = target * rows + rotated_slot % rows
-    pieces = 2
+    )(wide, inverse.reshape(-1), fine_attend_in, fine_attend_out)
+
+    pieces = count
     kinds = GROUP - 1
     second, pooled = pl.pallas_call(
         layer_two_kernel,
@@ -466,17 +477,16 @@
         in_specs=[VMEM, VMEM, SMEM, VMEM, VMEM, VMEM],
         out_specs=(VMEM, VMEM),
         scratch_shapes=[
-            pltpu.VMEM((row_size * rows, width), F32),
             pltpu.VMEM((BALL, width), F32),
             pltpu.VMEM((width // LANES, rows // pieces, LANES), F32),
             DMA((kinds, pieces)),
             DMA((kinds, pieces)),
         ],
         compiler_params=pltpu.CompilerParams(
-            collective_id=2, has_side_effects=True, vmem_limit_bytes=grant
+            collective_id=2, has_side_effects=True, vmem_limit_bytes=28 * mib
         ),
         name="layer_two",
-    )(first, turned, index, fine_gate_up[1], fine_down[1], pool_weight)
+    )(first, turned, route.reshape(-1), fine_gate_up, fine_down, pool_weight)
 
     return pl.pallas_call(
         coarse_kernel,
@@ -488,7 +498,7 @@
             pltpu.VMEM((GROUP * small, coarse_width), BF16),
             pltpu.VMEM((width // LANES, rows, LANES), F32),
         ],
-        compiler_params=pltpu.CompilerParams(vmem_limit_bytes=grant),
+        compiler_params=pltpu.CompilerParams(vmem_limit_bytes=36 * mib),
         name="coarse",
     )(
         pooled,

time: 133 us -> 117 us (0.88)
  Pallas kernels: 126 us -> 110 us
    pallas_call x1, Pallas kernels: 45.6 us -> 37 us  [local(): pl.pallas_call(layer_two_kernel, out_shape=(jax.ShapeDtypeStruct((rows, w...]
    unnamed x14 -> x28, local copies, waits for them, and re-layouts: 3.04 us -> 6.87 us
    pallas_call x1, Pallas kernels: 15.6 us -> 12.2 us  [local(): pl.pallas_call(coarse_kernel, out_shape=jax.ShapeDtypeStruct((rows, width...]
    squeeze x4 -> x0, local copies, waits for them, and re-layouts: 2.51 us -> none  [the longest x1 1.17 us: local(): fine_attend_in[1]]
    pallas_call x1, Pallas kernels: 32.1 us -> 29.9 us  [local(): pl.pallas_call(turn_kernel, out_shape=everyone, in_specs=[VMEM, SMEM, VME...]
    pallas_call x1, Pallas kernels: 32.6 us -> 30.6 us  [local(): pl.pallas_call(functools.partial(layer_one_kernel, col_size), out_shape=(...]
where the time goes in v1:
time: 117 us
  Pallas kernels  110 us (94%)
  local copies, waits for them, and re-layouts  6.87 us (6%)
    pallas_call x1, Pallas kernels, local(): pl.pallas_call(layer_two_kernel, out_shape=(jax.ShapeDtypeStruct((rows, w...  37 us
    pallas_call x1, Pallas kernels, local(): pl.pallas_call(functools.partial(layer_one_kernel, col_size), out_shape=(...  30.6 us
    pallas_call x1, Pallas kernels, local(): pl.pallas_call(turn_kernel, out_shape=everyone, in_specs=[VMEM, SMEM, VME...  29.9 us
    pallas_call x1, Pallas kernels, local(): pl.pallas_call(coarse_kernel, out_shape=jax.ShapeDtypeStruct((rows, width...  12.2 us
    unnamed x28, local copies, waits for them, and re-layouts  6.87 us

profile of v1, /device:TPU:0, one launch (start us, length us, event | category | flops | bytes accessed | tf_op | source)
XLA Modules:
  0.0 116.7 jit_solution(410999992449682096)
XLA Ops:
  0.0 0.0 copy-start
  0.0 1.6 %copy-done = bf16[2,256,2048]{2,1,0:T(8,128)(2,1)S(1)} copy-done((bf16[2,256,2048]{2,1,0:T(8,128)(2,1)S(1)}, bf16[2,256,2048]{2,1,0:T(8,128)(2,1)}, u32[]{:S(2)}) %copy-start) | copy-done | bytes 2097176
  1.6 0.0 copy-start.3
  1.6 1.2 %copy-done.3 = bf16[2,1024,256]{2,1,0:T(8,128)(2,1)S(1)} copy-done((bf16[2,1024,256]{2,1,0:T(8,128)(2,1)S(1)}, bf16[2,1024,256]{2,1,0:T(8,128)(2,1)}, u32[]{:S(2)}) %copy-start.3) | copy-done | bytes 1048600
  2.8 0.0 copy-start.5
  2.8 1.1 copy-done.5
  4.0 0.0 copy-start.10
  4.0 0.9 copy-done.10
  4.9 0.0 copy-start.11
  4.9 1.2 %copy-done.11 = bf16[2048,256]{1,0:T(8,128)(2,1)S(1)} copy-done((bf16[2048,256]{1,0:T(8,128)(2,1)S(1)}, bf16[2048,256]{1,0:T(8,128)(2,1)}, u32[]{:S(2)}) %copy-start.11) | copy-done | bytes 1048600
  6.1 0.0 copy-start.13
  6.1 0.7 copy-done.13
  6.8 30.6 %layer_one.1 = (bf16[2048,256]{1,0:T(8,128)(2,1)S(1)}, f32[8192,256]{1,0:T(8,128)S(1)}, s32[16,128]{1,0:T(8,128)S(1)}, s32[16,128]{1,0:T(8,128)S(1)}) custom-call(bf16[2048,256]{1,0:T(8,128)(2,1)S(1)} %copy-done.11, s32[16,128]{1,0:T(8,128)S(1)} %bitcast.3, bf16[2,256,768]{2,1,0:T(8,128)(2,1)S(1)} %copy-done.5, bf16[2,256,256]{2,1,0:T(8,128)(2,1)S(1)} %copy-done.10, ...), custom_call_target="tpu_custom_call" | custom-call | tf_op jit(solution)/shard_map/layer_one/pallas_call | solution.py:419
  37.4 0.0 copy-start.1
  37.5 0.0 copy-start.4
  37.5 0.0 copy-start.6
  37.5 29.9 %turn.1.wide = f32[8192,256]{1,0:T(8,128)S(1)} custom-call(f32[8192,256]{1,0:T(8,128)S(1)} %get-tuple-element.12.source, s32[2048]{0:T(1024)S(1)} %bitcast.5, bf16[2,256,768]{2,1,0:T(8,128)(2,1)S(1)} %copy-done.5, bf16[2,256,256]{2,1,0:T(8,128)(2,1)S(1)} %copy-done.10), custom_call_target="tpu_custom_call" | custom-call | tf_op jit(solution)/shard_map/turn/pallas_call | solution.py:452
  67.4 0.0 copy-done.1
  67.4 0.0 copy-done.4
  67.4 0.0 copy-done.6
  67.4 0.0 copy-start.2
  67.5 0.0 copy-start.7
  67.5 0.0 copy-start.8
  67.5 0.0 copy-start.9
  67.5 0.0 copy-start.12
  67.5 37.0 %layer_two.1 = (bf16[2048,256]{1,0:T(8,128)(2,1)S(1)}, bf16[8,256,512]{2,1,0:T(8,128)(2,1)S(1)}) custom-call(bf16[2048,256]{1,0:T(8,128)(2,1)S(1)} %get-tuple-element.11.first, f32[8192,256]{1,0:T(8,128)S(1)} %turn.1.wide, s32[2048]{0:T(1024)S(1)} %bitcast.4, bf16[2,256,2048]{2,1,0:T(8,128)(2,1)S(1)} %copy-done.1, bf16[2,1024,256]{2,1,0:T(8,128)(2,1)S(1)} %copy-done.4, ...), custom_call_target="tpu_custom_call" | custom-call | tf_op jit(solution)/shard_map/layer_two/pallas_call | solution.py:471
  104.5 0.0 copy-done.2
  104.5 0.0 copy-done.7
  104.5 0.0 copy-done.8
  104.5 0.0 copy-done.9
  104.5 0.0 copy-done.12
  104.5 12.2 %coarse.1 = bf16[2048,256]{1,0:T(8,128)(2,1)} custom-call(bf16[8,256,512]{2,1,0:T(8,128)(2,1)S(1)} %get-tuple-element.15.pooled, bf16[2048,256]{1,0:T(8,128)(2,1)S(1)} %get-tuple-element.16.second, bf16[512,1536]{1,0:T(8,128)(2,1)S(1)} %copy-done.9, bf16[512,512]{1,0:T(8,128)(2,1)S(1)} %copy-done.12, bf16[512,4096]{1,0:T(8,128)(2,1)S(1)} %copy-done.2, ...), custom_call_target="tpu_custom_call" | custom-call | tf_op jit(solution)/shard_map/coarse/pallas_call | solution.py:491
Async XLA Ops:
  0.0 1.6 %copy-start = (bf16[2,256,2048]{2,1,0:T(8,128)(2,1)S(1)}, bf16[2,256,2048]{2,1,0:T(8,128)(2,1)}, u32[]{:S(2)}) copy-start(bf16[2,256,2048]{2,1,0:T(8,128)(2,1)} %gate_up.4) | copy-start | bytes 6291460
  1.6 1.2 %copy-start.3 = (bf16[2,1024,256]{2,1,0:T(8,128)(2,1)S(1)}, bf16[2,1024,256]{2,1,0:T(8,128)(2,1)}, u32[]{:S(2)}) copy-start(bf16[2,1024,256]{2,1,0:T(8,128)(2,1)} %down.4) | copy-start | bytes 3145732
  2.8 1.1 copy-start.5
  4.0 0.9 copy-start.10
  4.9 1.2 %copy-start.11 = (bf16[2048,256]{1,0:T(8,128)(2,1)S(1)}, bf16[2048,256]{1,0:T(8,128)(2,1)}, u32[]{:S(2)}) copy-start(bf16[2048,256]{1,0:T(8,128)(2,1)} %points.1) | copy-start | bytes 3145732
  6.1 0.7 copy-start.13
  37.4 30.0 %copy-start.1 = (bf16[2,256,2048]{2,1,0:T(8,128)(2,1)S(1)}, bf16[2,256,2048]{2,1,0:T(8,128)(2,1)}, u32[]{:S(2)}) copy-start(bf16[2,256,2048]{2,1,0:T(8,128)(2,1)} %gate_up.4) | copy-start | bytes 6291460
  37.5 30.0 %copy-start.4 = (bf16[2,1024,256]{2,1,0:T(8,128)(2,1)S(1)}, bf16[2,1024,256]{2,1,0:T(8,128)(2,1)}, u32[]{:S(2)}) copy-start(bf16[2,1024,256]{2,1,0:T(8,128)(2,1)} %down.4) | copy-start | bytes 3145732
  37.5 30.0 %copy-start.6 = (bf16[2048,512]{1,0:T(8,128)(2,1)S(1)}, bf16[2048,512]{1,0:T(8,128)(2,1)}, u32[]{:S(2)}) copy-start(bf16[2048,512]{1,0:T(8,128)(2,1)} %pool.1) | copy-start | bytes 6291460
  67.4 37.0 %copy-start.2 = (bf16[512,4096]{1,0:T(8,128)(2,1)S(1)}, bf16[512,4096]{1,0:T(8,128)(2,1)}, u32[]{:S(2)}) copy-start(bf16[512,4096]{1,0:T(8,128)(2,1)} %gate_up.5) | copy-start | bytes 12582916
  67.5 37.0 %copy-start.7 = (bf16[2048,512]{1,0:T(8,128)(2,1)S(1)}, bf16[2048,512]{1,0:T(8,128)(2,1)}, u32[]{:S(2)}) copy-start(bf16[2048,512]{1,0:T(8,128)(2,1)} %down.5) | copy-start | bytes 6291460
  67.5 37.0 %copy-start.8 = (bf16[512,2048]{1,0:T(8,128)(2,1)S(1)}, bf16[512,2048]{1,0:T(8,128)(2,1)}, u32[]{:S(2)}) copy-start(bf16[512,2048]{1,0:T(8,128)(2,1)} %unpool.1) | copy-start | bytes 6291460
  67.5 37.0 %copy-start.9 = (bf16[512,1536]{1,0:T(8,128)(2,1)S(1)}, bf16[512,1536]{1,0:T(8,128)(2,1)}, u32[]{:S(2)}) copy-start(bf16[512,1536]{1,0:T(8,128)(2,1)} %w_in.5) | copy-start | bytes 4718596
  67.5 37.0 %copy-start.12 = (bf16[512,512]{1,0:T(8,128)(2,1)S(1)}, bf16[512,512]{1,0:T(8,128)(2,1)}, u32[]{:S(2)}) copy-start(bf16[512,512]{1,0:T(8,128)(2,1)} %w_out.5) | copy-start | bytes 1572868

commit v2 on v1

--- a/solution.py
+++ b/solution.py
@@ -160,19 +160,35 @@
 
 
 def layer_one_kernel(
-    col_size, points, slots, w_in, w_out, gate_up, down, out, wide, inverse, route, held,
-    slot_all, send, recv, s_send, s_recv,
+    col_size, points_hbm, slots_hbm, w_in_hbm, w_out_hbm, gate_up_hbm, down_hbm, out, wide,
+    inverse, route, held, slot_all, points, w_in, w_out, gate_up, down, loaded, send, recv,
+    s_send, s_recv,
 ):
     rows = points.shape[0]
     count = rows // BALL
     me, near, far = row_peers()
     other = far + near - me
+    loads = [
+        pltpu.make_async_copy(source, target, loaded.at[i])
+        for i, (source, target) in enumerate(
+            (
+                (slots_hbm, slot_all.at[me]),
+                (points_hbm, points),
+                (w_in_hbm.at[0], w_in),
+                (w_out_hbm.at[0], w_out),
+                (gate_up_hbm.at[0], gate_up),
+                (down_hbm.at[0], down),
+            )
+        )
+    ]
+    for load in loads:
+        load.start()
     greet((near, far, other), "row")
-    slot_all[me] = slots[...]
+    loads[0].wait()
 
     def slot_copy(kind, block, peer):
         return pltpu.make_async_remote_copy(
-            src_ref=slots,
+            src_ref=slot_all.at[me],
             dst_ref=slot_all.at[block],
             send_sem=s_send.at[kind],
             recv_sem=s_recv.at[kind],
@@ -182,13 +198,16 @@
 
     for kind, peer in enumerate((near, far, other)):
         slot_copy(kind, me, peer).start()
-    route[...] = slots[...] // (rows * col_size) * rows + slots[...] % rows
+    slots = slot_all[me]
+    route[...] = slots // (rows * col_size) * rows + slots % rows
+    for load in loads[1:]:
+        load.wait()
     gather = RowGather(held, wide, BALL, send, recv)
 
     def step(b, carry):
         u = points[pl.ds(b * BALL, BALL), :]
-        mixed = (u.astype(F32) + fine_attention(u, w_in[0], w_out[0])).astype(BF16)
-        value = ff_sum(mixed, gate_up[0], down[0]).astype(BF16)
+        mixed = (u.astype(F32) + fine_attention(u, w_in[...], w_out[...])).astype(BF16)
+        value = ff_sum(mixed, gate_up[...], down[...]).astype(BF16)
         out[pl.ds(pl.multiple_of(b * BALL, BALL), BALL), :] = value
         gather.own(b, value)
         gather.inside(b)
@@ -197,7 +216,7 @@
     lax.fori_loop(0, count, step, 0)
     for kind, peer in enumerate((near, far, other)):
         slot_copy(kind, peer, peer).wait()
-    lines, lanes = slots.shape
+    lines, lanes = slot_all.shape[1:]
     row_id = lax.broadcasted_iota(jnp.int32, (lines, lanes), 0)
     lane_id = lax.broadcasted_iota(jnp.int32, (lines, lanes), 1).astype(F32)
     sub_id = lax.broadcasted_iota(jnp.int32, (lanes, lanes), 0)
@@ -252,7 +271,8 @@
 
 
 def layer_two_kernel(
-    first, wide, index, gate_up, down, pool, second, pooled, taken, tall, send, recv
+    first, wide, index, gate_up, down, pool, w_in, second, own, queries, keys, values, pooled,
+    taken, tall, send, recv
 ):
     rows = second.shape[0]
     count = rows // BALL
@@ -324,34 +344,62 @@
         return carry
 
     lax.fori_loop(0, pieces, step, 0)
-    lax.fori_loop(max(pieces - COL_LAG, 0), pieces, relay, 0)
+    width = pool.shape[1]
+    block_rows = pooled.shape[1]
+    half = block_rows // 2
+
+    def project(block, at, size):
+        packed = dot(normed(pooled[block, at:at + size, :]), w_in[:, width:]).astype(BF16)
+        spot = pl.ds(pl.multiple_of(block * block_rows + at, size), size)
+        keys[spot, :] = packed[:, :width]
+        values[spot, :] = packed[:, width:]
+
+    def arrived(kind, block):
+        def one(c, carry):
+            copy(kind, c, block, flip).wait_recv()
+            return carry
+
+        lax.fori_loop(0, pieces, one, 0)
+
+    direct = [source_of(kind) for kind in range(1, lead)]
+    own[...] = pooled[me]
+    queries[...] = dot(normed(pooled[me]), w_in[:, :width]).astype(BF16)
+    project(me, 0, block_rows)
+    start = max(pieces - COL_LAG, 0)
+    for c in range(start, pieces):
+        relay(c, 0)
+        if c == start:
+            arrived(0, flip)
+            project(flip, 0, block_rows)
+        if c == start + 1:
+            for block in direct:
+                project(block, 0, half)
+    for block in direct:
+        project(block, half, half)
+    for kind in range(1, lead):
+        origin = source_of(kind)
+        block = origin + 1 - 2 * (origin % 2)
+        arrived(lead - 1 + kind, block)
+        project(block, 0, block_rows)
 
     def end(c, carry):
         copy(0, c, me, flip).wait_send()
-        copy(0, c, flip, flip).wait_recv()
         for kind in range(1, lead):
             copy(kind, c, me, peers[kind - 1]).wait_send()
             copy(lead - 1 + kind, c, source_of(kind), flip).wait_send()
-            origin = source_of(kind)
-            copy(lead - 1 + kind, c, origin + 1 - 2 * (origin % 2), flip).wait_recv()
         return carry
 
     lax.fori_loop(0, pieces, end, 0)
 
 
 def coarse_kernel(
-    pooled, second, w_in, w_out, gate_up, down, unpool, out, keys, values, lifted
+    pooled, queries, keys, values, second, w_out, gate_up, down, unpool, out, lifted
 ):
-    me = lax.axis_index("col") % GROUP
-    own = pooled[me]
+    own = pooled[...]
     rows, width = own.shape
     size = width // CHEADS
     factor = size ** -0.5 * LOG2E
-    for block in range(GROUP):
-        packed = dot(normed(pooled[block]), w_in[:, width:]).astype(BF16)
-        keys[pl.ds(block * rows, rows), :] = packed[:, :width]
-        values[pl.ds(block * rows, rows), :] = packed[:, width:]
-    q = dot(normed(own), w_in[:, :width]).astype(BF16)
+    q = queries[...]
     part = 256
     head_of = lax.broadcasted_iota(jnp.int32, (rows, part), 1) // size
     zero = jnp.zeros((), BF16)
@@ -419,18 +467,17 @@
     first, wide, inverse, route = pl.pallas_call(
         functools.partial(layer_one_kernel, col_size),
         out_shape=(jax.ShapeDtypeStruct((rows, width), BF16), everyone, scalars, scalars),
-        in_specs=[
-            VMEM,
-            VMEM,
-            VMEM,
-            VMEM,
-            VMEM,
-            VMEM,
-        ],
+        in_specs=[pl.BlockSpec(memory_space=pltpu.HBM)] * 6,
         out_specs=(VMEM,) * 4,
         scratch_shapes=[
             held,
             pltpu.VMEM((row_size, lines, lanes), jnp.int32),
+            pltpu.VMEM(points.shape, BF16),
+            pltpu.VMEM(fine_attend_in.shape[1:], BF16),
+            pltpu.VMEM(fine_attend_out.shape[1:], BF16),
+            pltpu.VMEM(fine_gate_up.shape[1:], BF16),
+            pltpu.VMEM(fine_down.shape[1:], BF16),
+            DMA((6,)),
             DMA((3, count)),
             DMA((3, count)),
             DMA((3,)),
@@ -441,12 +488,17 @@
         ),
         name="layer_one",
     )(
-        points,
-        rotated_slot.reshape(lines, lanes),
-        fine_attend_in,
-        fine_attend_out,
-        fine_gate_up,
-        fine_down,
+        *(
+            pltpu.with_memory_space_constraint(array, pltpu.HBM)
+            for array in (
+                points,
+                rotated_slot.reshape(lines, lanes),
+                fine_attend_in,
+                fine_attend_out,
+                fine_gate_up,
+                fine_down,
+            )
+        )
     )
 
     turned = pl.pallas_call(
@@ -461,49 +513,52 @@
             DMA((3, count)),
         ],
         compiler_params=pltpu.CompilerParams(
-            collective_id=1, has_side_effects=True, vmem_limit_bytes=32 * mib
+            collective_id=1, has_side_effects=True, vmem_limit_bytes=24 * mib
         ),
         name="turn",
     )(wide, inverse.reshape(-1), fine_attend_in, fine_attend_out)
 
     pieces = count
     kinds = GROUP - 1
-    second, pooled = pl.pallas_call(
+    one = jax.ShapeDtypeStruct((small, coarse_width), BF16)
+    every = jax.ShapeDtypeStruct((GROUP * small, coarse_width), BF16)
+    second, *coarse_parts = pl.pallas_call(
         layer_two_kernel,
         out_shape=(
             jax.ShapeDtypeStruct((rows, width), BF16),
-            jax.ShapeDtypeStruct((GROUP, small, coarse_width), BF16),
+            one,
+            one,
+            every,
+            every,
         ),
-        in_specs=[VMEM, VMEM, SMEM, VMEM, VMEM, VMEM],
-        out_specs=(VMEM, VMEM),
+        in_specs=[VMEM, VMEM, SMEM, VMEM, VMEM, VMEM, VMEM],
+        out_specs=(VMEM,) * 5,
         scratch_shapes=[
+            pltpu.VMEM((GROUP, small, coarse_width), BF16),
             pltpu.VMEM((BALL, width), F32),
             pltpu.VMEM((width // LANES, rows // pieces, LANES), F32),
             DMA((kinds, pieces)),
             DMA((kinds, pieces)),
         ],
         compiler_params=pltpu.CompilerParams(
-            collective_id=2, has_side_effects=True, vmem_limit_bytes=28 * mib
+            collective_id=2, has_side_effects=True, vmem_limit_bytes=20 * mib
         ),
         name="layer_two",
-    )(first, turned, route.reshape(-1), fine_gate_up, fine_down, pool_weight)
+    )(first, turned, route.reshape(-1), fine_gate_up, fine_down, pool_weight, coarse_attend_in)
 
     return pl.pallas_call(
         coarse_kernel,
         out_shape=jax.ShapeDtypeStruct((rows, width), BF16),
-        in_specs=[VMEM] * 7,
+        in_specs=[VMEM] * 9,
         out_specs=VMEM,
         scratch_shapes=[
-            pltpu.VMEM((GROUP * small, coarse_width), BF16),
-            pltpu.VMEM((GROUP * small, coarse_width), BF16),
             pltpu.VMEM((width // LANES, rows, LANES), F32),
         ],
-        compiler_params=pltpu.CompilerParams(vmem_limit_bytes=36 * mib),
+        compiler_params=pltpu.CompilerParams(vmem_limit_bytes=22 * mib),
         name="coarse",
     )(
-        pooled,
+        *coarse_parts,
         second,
-        coarse_attend_in,
         coarse_attend_out,
         coarse_gate_up,
         coarse_down,

time: 117 us -> 110 us (0.940)
  local copies, waits for them, and re-layouts: 6.87 us -> 0.06 us
    unnamed x28 -> x20, local copies, waits for them, and re-layouts: 6.87 us -> 0.06 us
    pallas_call x1, Pallas kernels: 12.2 us -> 9.83 us  [local(): pl.pallas_call(coarse_kernel, out_shape=jax.ShapeDtypeStruct((rows, width...]
    pallas_call x1, Pallas kernels: 30.6 us -> 31.9 us  [local(): pl.pallas_call(functools.partial(layer_one_kernel, col_size), out_shape=(...]
where the time goes in v2:
time: 110 us
  Pallas kernels  109 us (99%)
    pallas_call x1, Pallas kernels, local(): pl.pallas_call(layer_two_kernel, out_shape=(jax.ShapeDtypeStruct((rows, w...  37.8 us
    pallas_call x1, Pallas kernels, local(): pl.pallas_call(functools.partial(layer_one_kernel, col_size), out_shape=(...  31.9 us
    pallas_call x1, Pallas kernels, local(): pl.pallas_call(turn_kernel, out_shape=everyone, in_specs=[VMEM, SMEM, VME...  29.9 us
    pallas_call x1, Pallas kernels, local(): pl.pallas_call(coarse_kernel, out_shape=jax.ShapeDtypeStruct((rows, width...  9.83 us

profile of v2, /device:TPU:0, one launch (start us, length us, event | category | flops | bytes accessed | tf_op | source)
XLA Modules:
  0.0 109.7 jit_solution(10693514913258191420)
XLA Ops:
  0.0 0.0 copy-start.3
  0.0 0.0 copy-start.8
  0.0 31.9 %layer_one.1 = (bf16[2048,256]{1,0:T(8,128)(2,1)S(1)}, f32[8192,256]{1,0:T(8,128)S(1)}, s32[16,128]{1,0:T(8,128)S(1)}, s32[16,128]{1,0:T(8,128)S(1)}) custom-call(bf16[2048,256]{1,0:T(8,128)(2,1)} %points_hbm.1, s32[16,128]{1,0:T(8,128)} %bitcast.5, bf16[2,256,768]{2,1,0:T(8,128)(2,1)} %w_in.2, bf16[2,256,256]{2,1,0:T(8,128)(2,1)} %w_out.2, ...), custom_call_target="tpu_custom_call" | custom-call | tf_op jit(solution)/shard_map/layer_one/pallas_call | solution.py:467
  31.9 0.0 copy-done.3
  31.9 0.0 copy-done.8
  31.9 0.0 copy-start
  31.9 0.0 copy-start.1
  31.9 0.0 copy-start.4
  32.0 0.0 copy-start.7
  32.0 29.9 %turn.1.wide = f32[8192,256]{1,0:T(8,128)S(1)} custom-call(f32[8192,256]{1,0:T(8,128)S(1)} %get-tuple-element.15.source, s32[2048]{0:T(1024)S(1)} %bitcast.4, bf16[2,256,768]{2,1,0:T(8,128)(2,1)S(1)} %copy-done.3, bf16[2,256,256]{2,1,0:T(8,128)(2,1)S(1)} %copy-done.8), custom_call_target="tpu_custom_call" | custom-call | tf_op jit(solution)/shard_map/turn/pallas_call | solution.py:504
  61.9 0.0 copy-done
  61.9 0.0 copy-done.1
  61.9 0.0 copy-done.4
  61.9 0.0 copy-done.7
  61.9 0.0 copy-start.2
  62.0 0.0 copy-start.5
  62.0 0.0 copy-start.6
  62.0 0.0 copy-start.9
  62.0 37.8 %layer_two.1 = (bf16[2048,256]{1,0:T(8,128)(2,1)S(1)}, bf16[256,512]{1,0:T(8,128)(2,1)S(1)}, bf16[256,512]{1,0:T(8,128)(2,1)S(1)}, bf16[2048,512]{1,0:T(8,128)(2,1)S(1)}, bf16[2048,512]{1,0:T(8,128)(2,1)S(1)}) custom-call(bf16[2048,256]{1,0:T(8,128)(2,1)S(1)} %get-tuple-element.14.first, f32[8192,256]{1,0:T(8,128)S(1)} %turn.1.wide, s32[2048]{0:T(1024)S(1)} %bitcast.3, ...), custom_call_target="tpu_custom_call" | custom-call | tf_op jit(solution)/shard_map/layer_two/pallas_call | solution.py:525
  99.8 0.0 copy-done.2
  99.8 0.0 copy-done.5
  99.8 0.0 copy-done.6
  99.8 0.0 copy-done.9
  99.8 9.8 %coarse.1 = bf16[2048,256]{1,0:T(8,128)(2,1)} custom-call(bf16[256,512]{1,0:T(8,128)(2,1)S(1)} %get-tuple-element.18.pooled, bf16[256,512]{1,0:T(8,128)(2,1)S(1)} %get-tuple-element.19.queries, bf16[2048,512]{1,0:T(8,128)(2,1)S(1)} %get-tuple-element.20.keys, bf16[2048,512]{1,0:T(8,128)(2,1)S(1)} %get-tuple-element.21.values, ...), custom_call_target="tpu_custom_call" | custom-call | tf_op jit(solution)/shard_map/coarse/pallas_call | solution.py:549
Async XLA Ops:
  0.0 31.9 %copy-start.3 = (bf16[2,256,768]{2,1,0:T(8,128)(2,1)S(1)}, bf16[2,256,768]{2,1,0:T(8,128)(2,1)}, u32[]{:S(2)}) copy-start(bf16[2,256,768]{2,1,0:T(8,128)(2,1)} %w_in.2) | copy-start | bytes 2359300
  0.0 31.9 %copy-start.8 = (bf16[2,256,256]{2,1,0:T(8,128)(2,1)S(1)}, bf16[2,256,256]{2,1,0:T(8,128)(2,1)}, u32[]{:S(2)}) copy-start(bf16[2,256,256]{2,1,0:T(8,128)(2,1)} %w_out.2) | copy-start | bytes 786436
  31.9 30.0 %copy-start = (bf16[2,256,2048]{2,1,0:T(8,128)(2,1)S(1)}, bf16[2,256,2048]{2,1,0:T(8,128)(2,1)}, u32[]{:S(2)}) copy-start(bf16[2,256,2048]{2,1,0:T(8,128)(2,1)} %gate_up.2) | copy-start | bytes 6291460
  31.9 30.0 %copy-start.1 = (bf16[2,1024,256]{2,1,0:T(8,128)(2,1)S(1)}, bf16[2,1024,256]{2,1,0:T(8,128)(2,1)}, u32[]{:S(2)}) copy-start(bf16[2,1024,256]{2,1,0:T(8,128)(2,1)} %down.2) | copy-start | bytes 3145732
  31.9 30.0 %copy-start.4 = (bf16[2048,512]{1,0:T(8,128)(2,1)S(1)}, bf16[2048,512]{1,0:T(8,128)(2,1)}, u32[]{:S(2)}) copy-start(bf16[2048,512]{1,0:T(8,128)(2,1)} %pool.1) | copy-start | bytes 6291460
  32.0 30.0 %copy-start.7 = (bf16[512,1536]{1,0:T(8,128)(2,1)S(1)}, bf16[512,1536]{1,0:T(8,128)(2,1)}, u32[]{:S(2)}) copy-start(bf16[512,1536]{1,0:T(8,128)(2,1)} %w_in.3) | copy-start | bytes 4718596
  61.9 37.8 %copy-start.2 = (bf16[512,4096]{1,0:T(8,128)(2,1)S(1)}, bf16[512,4096]{1,0:T(8,128)(2,1)}, u32[]{:S(2)}) copy-start(bf16[512,4096]{1,0:T(8,128)(2,1)} %gate_up.3) | copy-start | bytes 12582916
  62.0 37.8 %copy-start.5 = (bf16[2048,512]{1,0:T(8,128)(2,1)S(1)}, bf16[2048,512]{1,0:T(8,128)(2,1)}, u32[]{:S(2)}) copy-start(bf16[2048,512]{1,0:T(8,128)(2,1)} %down.3) | copy-start | bytes 6291460
  62.0 37.8 %copy-start.6 = (bf16[512,2048]{1,0:T(8,128)(2,1)S(1)}, bf16[512,2048]{1,0:T(8,128)(2,1)}, u32[]{:S(2)}) copy-start(bf16[512,2048]{1,0:T(8,128)(2,1)} %unpool.1) | copy-start | bytes 6291460
  62.0 37.8 %copy-start.9 = (bf16[512,512]{1,0:T(8,128)(2,1)S(1)}, bf16[512,512]{1,0:T(8,128)(2,1)}, u32[]{:S(2)}) copy-start(bf16[512,512]{1,0:T(8,128)(2,1)} %w_out.3) | copy-start | bytes 1572868
